TPU v7x, 128 devices: a whole 4x4x4 slice. The times are simulated.
128 devices in a mesh: rows: 32 (over z, x, core), rep: 4 (over y).
Axes of the slice: x: 4, y: 4, z: 4, core: 2. Of those that a mesh axis runs over, the one named last changes fastest.
Arguments:
- features: bfloat16 [65536, 512], P(('rows', 'rep')), may hold values from -6 to 6
- weight: bfloat16 [512, 512], replicated, may hold values from -6 to 6
- out_bias: float32 [512], replicated, may hold values from -4 to 4
- degree: int32 [65536], P(('rows', 'rep')), may hold values from 256 to 1023
- tile_row: int32 [8192], P(('rows', 'rep')), may hold values from 0 to 15, as said below
- tile_col: int32 [8192], P(('rows', 'rep')), may hold values from 0 to 127, as said below
- tile_value: bfloat16 [8192, 128, 128], P(('rows', 'rep')), may hold values from 0 to 3, as said below
- cotangent: bfloat16 [65536, 512], P(('rows', 'rep')), may hold values from -6 to 6
Outputs:
- hidden_out: bfloat16 [65536, 512], P(('rows', 'rep'))
- grad_input: bfloat16 [65536, 512], P(('rows', 'rep'))
- grad_weight: float32 [512, 512], replicated
Inputs may be any that keep to these rules, and one draw needn't show every extreme that they name: `tile_row`: on each device the slots that hold edges come first; every later slot has an all-zero tile and both of its indices 0. Every node block's diagonal block is among its device's slots. Columns of a device's group are numbered slab by slab: tile_col = j * 4 + b names node block (j * 4 + c) * 4 + b. `tile_value`: all slots together form a symmetric adjacency: for every slot with tile V on global blocks (g, h) there is a slot on (h, g) with tile V transposed, and a diagonal block's tile is symmetric. Entries are 0 or between 0.1 and 3.
All inputs are finite; a program needn't handle non-finite values.
Results may differ from a plain program's by a relative error of at most 0.0061.
Values may be sent and summed in bfloat16 or wider, within the bound.
A program may use at most 128 MiB of HBM per device.

v0:
```python
import jax
import jax.numpy as jnp
from jax import lax
from jax.sharding import PartitionSpec as P


def aggregate_slots(panels, group_rows_all, group_cols_all, tiles_all, out_blocks):
    tile_size = tiles_all.shape[1]
    feat_width = panels.shape[1]
    panel_blocks = panels.reshape(-1, tile_size, feat_width)
    group_count = tiles_all.shape[0] // 8

    def add_group(totals, bundle):
        group_rows, group_cols, group_tiles = bundle
        products = jnp.einsum(
            "sij,sjf->sif",
            group_tiles,
            panel_blocks[group_cols],
            preferred_element_type=jnp.float32,
        )
        return (totals.at[group_rows].add(products), None)

    initial = jnp.zeros((out_blocks, tile_size, feat_width), jnp.float32)
    bundles = (
        group_rows_all.reshape(group_count, 8),
        group_cols_all.reshape(group_count, 8),
        tiles_all.reshape(group_count, 8, tile_size, tile_size),
    )
    totals, _ = lax.scan(add_group, initial, bundles)
    return totals.reshape(out_blocks * tile_size, feat_width)


def shards(features, weight, out_bias, degree, tile_row, tile_col, tile_value, cotangent):
    tile_size = tile_value.shape[1]
    nodes_dev = features.shape[0]
    feat_width = features.shape[1]
    block_count = nodes_dev // tile_size
    rep_count = lax.axis_size("rep")
    row_scale = lax.rsqrt(degree.astype(jnp.float32))[:, None]
    scaled = (jnp.dot(features, weight, preferred_element_type=jnp.float32) * row_scale).astype(
        jnp.bfloat16
    )
    panels = lax.all_gather(scaled, "rows", axis=0, tiled=True)
    slab_part = aggregate_slots(panels, tile_row, tile_col, tile_value, rep_count * block_count)
    aggregate = lax.psum_scatter(slab_part, "rep", scatter_dimension=0, tiled=True) * row_scale
    pre_act = aggregate + out_bias
    hidden_out = jax.nn.silu(pre_act).astype(jnp.bfloat16)
    sigmoid_pre = jax.nn.sigmoid(pre_act)
    grad_pre = cotangent.astype(jnp.float32) * sigmoid_pre * (1.0 + pre_act * (1.0 - sigmoid_pre))
    scaled_grad = (grad_pre * row_scale).astype(jnp.bfloat16)
    slab_grads = lax.all_gather(scaled_grad, "rep", axis=0, tiled=True)
    grad_blocks = slab_grads.reshape(rep_count * block_count, tile_size, feat_width)
    products = jnp.einsum(
        "sji,sjf->sif", tile_value, grad_blocks[tile_row], preferred_element_type=jnp.float32
    )
    block_total = nodes_dev * lax.axis_size("rows") // tile_size
    target = jnp.where((tile_col >= 0) & (tile_col < block_total), tile_col, block_total)
    totals = jnp.zeros((block_total, tile_size, feat_width), jnp.float32)
    totals = totals.at[target].add(products, mode="drop")
    back_total = lax.psum_scatter(
        totals.reshape(nodes_dev * lax.axis_size("rows"), feat_width),
        "rows",
        scatter_dimension=0,
        tiled=True,
    )
    back_sum = (back_total * row_scale).astype(jnp.bfloat16)
    grad_input = lax.dot_general(
        back_sum, weight, (((1,), (1,)), ((), ())), preferred_element_type=jnp.float32
    ).astype(jnp.bfloat16)
    local_weight = lax.dot_general(
        features, back_sum, (((0,), (0,)), ((), ())), preferred_element_type=jnp.float32
    )
    grad_weight = lax.psum(local_weight, ("rows", "rep"))
    return (hidden_out, grad_input, grad_weight)


def solution(mesh):
    placed = (
        P(("rows", "rep"), None),
        P(),
        P(),
        P(("rows", "rep")),
        P(("rows", "rep")),
        P(("rows", "rep")),
        P(("rows", "rep"), None, None),
        P(("rows", "rep"), None),
    )
    return jax.shard_map(
        shards,
        mesh=mesh,
        in_specs=placed,
        out_specs=(P(("rows", "rep"), None), P(("rows", "rep"), None), P()),
        check_vma=False,
    )
```

profile of v0, /device:TPU:1, one launch (start us, length us, event | category | flops | bytes accessed | tf_op | source)
XLA Modules:
  0.0 688.1 jit_solution(9885065440772527485)
XLA Ops:
  7.2 0.0 copy-start
  7.2 0.0 all-gather.3.cloned.1.call-start
  7.2 0.7 convert_rsqrt_fusion
  8.0 0.3 copy-done
  8.2 2.3 fusion.8
  10.5 0.0 all-gather.3.cloned.1.call-update
  10.5 0.0 reduce-scatter.3.cloned.1.call-start
  10.6 0.7 reshape.85
  11.3 0.7 reshape.87
  12.0 75.1 %all-gather.3.cloned.1.call-done = bf16[16384,512]{1,0:T(8,128)(2,1)} async-done(((bf16[512,512]{1,0:T(8,128)(2,1)}), bf16[16384,512]{1,0:T(8,128)(2,1)}) %all-gather.3.cloned.1.call-update) | async-done | bytes 16777232 | tf_op jit(solution)/shard_map/all_gather | solution.py:43
  87.1 2.5 broadcast_in_dim.18
  89.6 107.3 %while.10 = (s32[]{:T(128)}, f32[16,128,512]{2,1,0:T(8,128)}, s32[8,8]{1,0:T(8,128)S(1)}, bf16[8,8,128,128]{3,2,1,0:T(8,128)(2,1)}, s32[8,8]{1,0:T(8,128)S(1)}, /*index=5*/bf16[128,128,512]{2,1,0:T(8,128)(2,1)}, s32[]{:T(128)}) while((s32[]{:T(128)}, f32[16,128,512]{2,1,0:T(8,128)}, s32[8,8]{1,0:T(8,128)S(1)}, ...), condition=%wide.region_2.3_spmd, body=%wide.region_0.2_spmd.sunk | while | flops 134743088 | bytes 11800893 | solution.py:29
  89.6 7.4 %gather_fusion = bf16[8,128,512]{2,1,0:T(8,128)(2,1)} fusion(bf16[128,128,512]{2,1,0:T(8,128)(2,1)} %get-tuple-element.118, s32[1024]{0:T(1024)S(1)} %pad_clamp_fusion.3), kind=kCustom, calls=%fused_computation.clone.1 | custom fusion | bytes 2097184 | tf_op jit(solution)/shard_map/while/body/eval_jaxpr/gather | solution.py:18
  97.0 1.7 fusion.23
  98.7 4.4 scatter_fusion
  103.1 7.4 %gather_fusion = bf16[8,128,512]{2,1,0:T(8,128)(2,1)} fusion(bf16[128,128,512]{2,1,0:T(8,128)(2,1)} %get-tuple-element.118, s32[1024]{0:T(1024)S(1)} %pad_clamp_fusion.3), kind=kCustom, calls=%fused_computation.clone.1 | custom fusion | bytes 2097184 | tf_op jit(solution)/shard_map/while/body/eval_jaxpr/gather | solution.py:18
  110.5 1.7 fusion.23
  112.2 4.3 scatter_fusion
  116.5 7.4 %gather_fusion = bf16[8,128,512]{2,1,0:T(8,128)(2,1)} fusion(bf16[128,128,512]{2,1,0:T(8,128)(2,1)} %get-tuple-element.118, s32[1024]{0:T(1024)S(1)} %pad_clamp_fusion.3), kind=kCustom, calls=%fused_computation.clone.1 | custom fusion | bytes 2097184 | tf_op jit(solution)/shard_map/while/body/eval_jaxpr/gather | solution.py:18
  123.8 1.7 fusion.23
  125.6 4.1 scatter_fusion
  129.7 7.4 %gather_fusion = bf16[8,128,512]{2,1,0:T(8,128)(2,1)} fusion(bf16[128,128,512]{2,1,0:T(8,128)(2,1)} %get-tuple-element.118, s32[1024]{0:T(1024)S(1)} %pad_clamp_fusion.3), kind=kCustom, calls=%fused_computation.clone.1 | custom fusion | bytes 2097184 | tf_op jit(solution)/shard_map/while/body/eval_jaxpr/gather | solution.py:18
  137.0 1.7 fusion.23
  138.8 4.1 scatter_fusion
  142.9 7.4 %gather_fusion = bf16[8,128,512]{2,1,0:T(8,128)(2,1)} fusion(bf16[128,128,512]{2,1,0:T(8,128)(2,1)} %get-tuple-element.118, s32[1024]{0:T(1024)S(1)} %pad_clamp_fusion.3), kind=kCustom, calls=%fused_computation.clone.1 | custom fusion | bytes 2097184 | tf_op jit(solution)/shard_map/while/body/eval_jaxpr/gather | solution.py:18
  150.3 1.7 fusion.23
  152.0 4.2 scatter_fusion
  156.3 7.4 %gather_fusion = bf16[8,128,512]{2,1,0:T(8,128)(2,1)} fusion(bf16[128,128,512]{2,1,0:T(8,128)(2,1)} %get-tuple-element.118, s32[1024]{0:T(1024)S(1)} %pad_clamp_fusion.3), kind=kCustom, calls=%fused_computation.clone.1 | custom fusion | bytes 2097184 | tf_op jit(solution)/shard_map/while/body/eval_jaxpr/gather | solution.py:18
  163.6 1.7 fusion.23
  165.3 4.5 scatter_fusion
  169.8 7.4 %gather_fusion = bf16[8,128,512]{2,1,0:T(8,128)(2,1)} fusion(bf16[128,128,512]{2,1,0:T(8,128)(2,1)} %get-tuple-element.118, s32[1024]{0:T(1024)S(1)} %pad_clamp_fusion.3), kind=kCustom, calls=%fused_computation.clone.1 | custom fusion | bytes 2097184 | tf_op jit(solution)/shard_map/while/body/eval_jaxpr/gather | solution.py:18
  177.2 1.7 fusion.23
  178.9 4.5 scatter_fusion
  183.4 7.4 %gather_fusion = bf16[8,128,512]{2,1,0:T(8,128)(2,1)} fusion(bf16[128,128,512]{2,1,0:T(8,128)(2,1)} %get-tuple-element.118, s32[1024]{0:T(1024)S(1)} %pad_clamp_fusion.3), kind=kCustom, calls=%fused_computation.clone.1 | custom fusion | bytes 2097184 | tf_op jit(solution)/shard_map/while/body/eval_jaxpr/gather | solution.py:18
  190.7 1.7 fusion.23
  192.5 4.5 scatter_fusion
  196.9 0.0 copy-start.3
  196.9 0.0 reduce-scatter.3.cloned.1.call-update
  197.0 0.0 all-gather.5.cloned.1.call-start
  197.0 46.4 %reduce-scatter.3.cloned.1.call-done = f32[512,512]{1,0:T(8,128)} async-done(((f32[2048,512]{1,0:T(8,128)}), f32[512,512]{1,0:T(8,128)}) %reduce-scatter.3.cloned.1.call-update) | async-done | bytes 1048592 | tf_op jit(solution)/shard_map/reduce_scatter | solution.py:45
  243.5 0.0 copy-done.3
  243.5 0.0 copy-done.5
  243.5 2.8 multiply_convert_fusion.1
  246.2 0.0 all-gather.5.cloned.1.call-update
  246.3 0.0 reduce-scatter.5.cloned.1.call-start
  246.3 0.0 copy-done.6
  246.4 0.0 copy-done.7
  246.4 30.4 %all-gather.5.cloned.1.call-done = bf16[2048,512]{1,0:T(8,128)(2,1)} async-done(((bf16[512,512]{1,0:T(8,128)(2,1)}), bf16[2048,512]{1,0:T(8,128)(2,1)}) %all-gather.5.cloned.1.call-update) | async-done | bytes 2097168 | tf_op jit(solution)/shard_map/all_gather | solution.py:51
  276.8 7.2 %gather_fusion.1 = bf16[64,128,512]{2,1,0:T(8,128)(2,1)} fusion(bf16[16,128,512]{2,1,0:T(8,128)(2,1)} %bitcast.45, s32[1024]{0:T(1024)S(1)} %pad_clamp_fusion.1), kind=kCustom, calls=%fused_computation.1 | custom fusion | bytes 16777472 | tf_op jit(solution)/shard_map/gather | solution.py:54
  284.0 0.0 copy-done.1
  284.0 11.5 %convolution_bitcast_fusion = f32[64,128,512]{1,2,0:T(8,128)} fusion(bf16[64,128,512]{2,1,0:T(8,128)(2,1)} %gather_fusion.1, bf16[64,128,128]{2,1,0:T(8,128)(2,1)S(1)} %bitcast.47), kind=kOutput, calls=%fused_computation.17 | convolution fusion | flops 1073741824 | bytes 27262976 | tf_op jit(solution)/shard_map/sji,sjf->sif/dot_general | solution.py:53
  295.5 17.5 %copy.14 = f32[64,128,512]{2,1,0:T(8,128)} copy(f32[64,128,512]{1,2,0:T(8,128)} %convolution_bitcast_fusion) | data formatting | bytes 33554432 | tf_op jit(solution)/shard_map/sji,sjf->sif/dot_general | solution.py:53
  313.0 11.3 %broadcast_in_dim.19 = f32[128,128,512]{2,1,0:T(8,128)} broadcast(f32[]{:T(128)} %constant.5.clone.1), dimensions={} | broadcast | bytes 33554436 | tf_op jit(solution)/shard_map/broadcast_in_dim | solution.py:58
  324.3 36.3 %scatter_fusion.1 = f32[128,128,512]{2,1,0:T(8,128)} fusion(f32[128,128,512]{2,1,0:T(8,128)} %broadcast_in_dim.19, s32[64]{0:T(128)S(1)} %compare_select_fusion.3, f32[64,128,512]{2,1,0:T(8,128)} %copy.14), kind=kCustom, calls=%fused_computation.3 | custom fusion | flops 4194304 | bytes 50331904 | tf_op jit(solution)/shard_map/scatter-add | solution.py:59
  360.5 0.0 reduce-scatter.5.cloned.1.call-update
  360.6 0.0 all-reduce.2.cloned.1.call-start
  360.6 165.4 %reduce-scatter.5.cloned.1.call-done = f32[512,512]{1,0:T(8,128)} async-done(((f32[16384,512]{1,0:T(8,128)}), f32[512,512]{1,0:T(8,128)}) %reduce-scatter.5.cloned.1.call-update) | async-done | bytes 1048592 | tf_op jit(solution)/shard_map/reduce_scatter | solution.py:60
  526.1 2.8 convolution_bitcast_fusion.1
  528.9 0.0 all-reduce.2.cloned.1.call-update
  528.9 0.0 copy-done.4
  528.9 0.0 copy-done.2
  528.9 1.3 convolution_convert_fusion
  530.2 148.8 %all-reduce.2.cloned.1.call-done = f32[512,512]{0,1:T(8,128)} async-done(((f32[512,512]{0,1:T(8,128)}), f32[512,512]{0,1:T(8,128)}) %all-reduce.2.cloned.1.call-update) | async-done | bytes 1048592 | tf_op jit(solution)/shard_map/psum | solution.py:73
  679.1 2.5 copy.15
  (25 shorter events, 0.1 us)
Async XLA Ops:
  7.2 1.1 copy-start
  7.2 80.0 %all-gather.3.cloned.1.call-start = ((), (), s32[]{:S(2)}) async-start(), calls=%async_computation.2 | async-start | bytes 17301504 | tf_op jit(solution)/shard_map/all_gather | solution.py:43
  10.5 232.9 %reduce-scatter.3.cloned.1.call-start = ((), (), s32[]{:S(2)}) async-start(), calls=%async_computation.3 | async-start | bytes 5242880 | tf_op jit(solution)/shard_map/reduce_scatter | solution.py:45
  196.9 46.5 %copy-start.3 = (bf16[512,512]{1,0:T(8,128)(2,1)S(1)}, bf16[512,512]{1,0:T(8,128)(2,1)}, u32[]{:S(2)}) copy-start(bf16[512,512]{1,0:T(8,128)(2,1)} %param.17) | copy-start | bytes 1572868
  196.9 46.5 %copy-start.5 = (f32[512]{0:T(512)S(1)}, f32[512]{0:T(512)}, u32[]{:S(2)}) copy-start(f32[512]{0:T(512)} %param.12) | copy-start | bytes 6148
  196.9 49.4 %copy-start.6 = (s32[64]{0:T(128)S(1)}, s32[64]{0:T(128)}, u32[]{:S(2)}) copy-start(s32[64]{0:T(128)} %param.14) | copy-start | bytes 772
  196.9 49.4 %copy-start.7 = (s32[64]{0:T(128)S(1)}, s32[64]{0:T(128)}, u32[]{:S(2)}) copy-start(s32[64]{0:T(128)} %param.15) | copy-start | bytes 772
  197.0 79.9 %all-gather.5.cloned.1.call-start = ((), (), s32[]{:S(2)}) async-start(), calls=%async_computation.4 | async-start | bytes 2621440 | tf_op jit(solution)/shard_map/all_gather | solution.py:51
  246.3 279.8 %reduce-scatter.5.cloned.1.call-start = ((), (), s32[]{:S(2)}) async-start(), calls=%async_computation.5 | async-start | bytes 34603008 | tf_op jit(solution)/shard_map/reduce_scatter | solution.py:60
  276.8 7.2 %copy-start.1 = (bf16[8,8,128,128]{3,2,1,0:T(8,128)(2,1)S(1)}, bf16[8,8,128,128]{3,2,1,0:T(8,128)(2,1)}, u32[]{:S(2)}) copy-start(bf16[8,8,128,128]{3,2,1,0:T(8,128)(2,1)} %get-tuple-element.130) | copy-start | bytes 6291460
  360.5 168.4 %copy-start.4 = (bf16[512,512]{1,0:T(8,128)(2,1)S(1)}, bf16[512,512]{1,0:T(8,128)(2,1)}, u32[]{:S(2)}) copy-start(bf16[512,512]{1,0:T(8,128)(2,1)} %param.11) | copy-start | bytes 1572868
  360.6 318.5 %all-reduce.2.cloned.1.call-start = ((), (), s32[]{:S(2)}) async-start(), calls=%async_computation.6 | async-start | bytes 2097152 | tf_op jit(solution)/shard_map/psum | solution.py:73
  526.1 2.9 copy-start.2
Sparse Core Ops, SparseCore 0:
  10.8 76.2 all-gather.2
  197.1 46.3 reduce-scatter.2
  246.4 30.3 all-gather.4
  360.7 165.3 reduce-scatter.4
  531.3 147.7 all-reduce.1
where the time goes:
time: 690 us; the launch traced here: 688 us
  waiting for transfers between devices  466 us (68%)
  local copies, waits for them, and re-layouts  101 us (15%)
  other arithmetic  74.4 us (11%)
  matrix products  31.8 us (5%)
  between operations  13.9 us (2%)
    reduce_scatter x1, waiting for transfers between devices, shards(): lax.psum_scatter(totals.reshape(nodes_dev * lax.axis_size('rows'), feat_w...  165 us
    psum x1, waiting for transfers between devices, shards(): grad_weight = lax.psum(local_weight, ('rows', 'rep'))  149 us
    all_gather x1, waiting for transfers between devices, shards(): panels = lax.all_gather(scaled, 'rows', axis=0, tiled=True)  75.1 us
    gather x8, local copies, waits for them, and re-layouts, add_group(): panel_blocks[group_cols]  58.8 us
    reduce_scatter x1, waiting for transfers between devices, shards(): lax.psum_scatter(slab_part, 'rep', scatter_dimension=0, tiled=True)  46.4 us
    scatter-add x1, other arithmetic, shards(): totals = totals.at[target].add(products, mode='drop')  36.3 us
    scatter-add x8, other arithmetic, add_group(): return (totals.at[group_rows].add(products), None)  34.5 us
    all_gather x1, waiting for transfers between devices, shards(): slab_grads = lax.all_gather(scaled_grad, 'rep', axis=0, tiled=True)  30.4 us
  transfers between devices with their start and end apart: 5, of which 5 were waited for; matrix products, arithmetic and copies ran while one was open for 0% of the time, Pallas kernels for 0%

commit v1 on v0

--- a/solution.py
+++ b/solution.py
@@ -40,7 +40,15 @@
     scaled = (jnp.dot(features, weight, preferred_element_type=jnp.float32) * row_scale).astype(
         jnp.bfloat16
     )
-    panels = lax.all_gather(scaled, "rows", axis=0, tiled=True)
+    panels = jnp.concatenate(
+        lax.all_to_all(
+            jnp.stack(lax.axis_size("rows") * [scaled]),
+            concat_axis=0,
+            split_axis=0,
+            axis_name="rows",
+        ),
+        axis=0,
+    )
     slab_part = aggregate_slots(panels, tile_row, tile_col, tile_value, rep_count * block_count)
     aggregate = lax.psum_scatter(slab_part, "rep", scatter_dimension=0, tiled=True) * row_scale
     pre_act = aggregate + out_bias

time: 690 us -> 838 us (1.21)
  waiting for transfers between devices: 466 us -> 601 us
  starting transfers between devices: 0.21 us -> 9.77 us
    all_to_all x0 -> x1, waiting for transfers between devices: none -> 202 us  [shards(): lax.all_to_all(jnp.stack(lax.axis_size('rows') * [scaled]), concat_axis=0...]
    all_gather x1 -> x0, waiting for transfers between devices: 75.1 us -> none  [shards(): panels = lax.all_gather(scaled, 'rows', axis=0, tiled=True)]
    all_to_all x0 -> x1, starting transfers between devices: none -> 9.61 us  [shards(): lax.all_to_all(jnp.stack(lax.axis_size('rows') * [scaled]), concat_axis=0...]
    reduce_scatter x1, waiting for transfers between devices: 46.4 us -> 55 us  [shards(): lax.psum_scatter(slab_part, 'rep', scatter_dimension=0, tiled=True)]
where the time goes in v1:
time: 838 us; the launch traced here: 837 us
  waiting for transfers between devices  601 us (72%)
  local copies, waits for them, and re-layouts  106 us (13%)
  other arithmetic  74.2 us (9%)
  matrix products  32.1 us (4%)
  between operations  13.8 us (2%)
  starting transfers between devices  9.77 us (1%)
    all_to_all x1, waiting for transfers between devices, shards(): lax.all_to_all(jnp.stack(lax.axis_size('rows') * [scaled]), concat_axis=0...  202 us
    reduce_scatter x1, waiting for transfers between devices, shards(): lax.psum_scatter(totals.reshape(nodes_dev * lax.axis_size('rows'), feat_w...  165 us
    psum x1, waiting for transfers between devices, shards(): grad_weight = lax.psum(local_weight, ('rows', 'rep'))  148 us
    gather x8, local copies, waits for them, and re-layouts, add_group(): panel_blocks[group_cols]  58.9 us
    reduce_scatter x1, waiting for transfers between devices, shards(): lax.psum_scatter(slab_part, 'rep', scatter_dimension=0, tiled=True)  55 us
    scatter-add x1, other arithmetic, shards(): totals = totals.at[target].add(products, mode='drop')  36.1 us
    scatter-add x8, other arithmetic, add_group(): return (totals.at[group_rows].add(products), None)  34.4 us
    all_gather x1, waiting for transfers between devices, shards(): slab_grads = lax.all_gather(scaled_grad, 'rep', axis=0, tiled=True)  30.4 us
  transfers between devices with their start and end apart: 5, of which 5 were waited for; matrix products, arithmetic and copies ran while one was open for 0% of the time, Pallas kernels for 0%

profile of v1, /device:TPU:1, one launch (start us, length us, event | category | flops | bytes accessed | tf_op | source)
XLA Modules:
  0.0 836.7 jit_solution(15942530162691704051)
XLA Ops:
  7.2 0.0 copy-start
  7.2 0.7 convert_rsqrt_fusion
  7.9 0.3 copy-done
  8.2 1.5 fusion.8
  9.7 5.9 stack.2
  15.7 0.0 copy-start.5
  15.7 0.0 copy-start.6
  15.7 9.6 %all-to-all-start = ((bf16[32,512,512]{2,1,0:T(8,128)(2,1)}), bf16[32,512,512]{2,1,0:T(8,128)(2,1)}, u32[]{:S(2)}, u32[]{:S(2)}) async-start(bf16[32,512,512]{2,1,0:T(8,128)(2,1)} %stack.2), calls=%async_computation | async-start | bytes 33554432 | tf_op jit(solution)/shard_map/all_to_all | solution.py:44
  25.3 0.0 reduce-scatter.3.cloned.1.call-start
  25.3 0.0 copy-done.5
  25.3 0.1 reshape.84
  25.4 0.0 copy-done.6
  25.4 0.1 reshape.86
  25.5 201.9 %all-to-all-done = bf16[32,512,512]{2,1,0:T(8,128)(2,1)} async-done(((bf16[32,512,512]{2,1,0:T(8,128)(2,1)}), bf16[32,512,512]{2,1,0:T(8,128)(2,1)}, u32[]{:S(2)}, u32[]{:S(2)}) %all-to-all-start) | async-done | bytes 16777248 | tf_op jit(solution)/shard_map/all_to_all | solution.py:44
  227.3 2.5 broadcast_in_dim.18
  229.8 107.2 %while.10 = (s32[]{:T(128)}, f32[16,128,512]{2,1,0:T(8,128)}, s32[8,8]{1,0:T(8,128)S(1)}, bf16[8,8,128,128]{3,2,1,0:T(8,128)(2,1)}, s32[8,8]{1,0:T(8,128)S(1)}, /*index=5*/bf16[128,128,512]{2,1,0:T(8,128)(2,1)}, s32[]{:T(128)}) while((s32[]{:T(128)}, f32[16,128,512]{2,1,0:T(8,128)}, s32[8,8]{1,0:T(8,128)S(1)}, ...), condition=%wide.region_2.3_spmd, body=%wide.region_0.2_spmd.sunk | while | flops 134743088 | bytes 11800893 | solution.py:29
  229.8 7.4 gather_fusion
  237.2 1.7 fusion.23
  239.0 4.4 scatter_fusion
  243.4 7.4 gather_fusion
  250.7 1.7 fusion.23
  252.4 4.3 scatter_fusion
  256.7 7.4 gather_fusion
  264.1 1.7 fusion.23
  265.8 4.1 scatter_fusion
  270.0 7.4 gather_fusion
  277.3 1.7 fusion.23
  279.0 4.1 scatter_fusion
  283.2 7.4 gather_fusion
  290.6 1.7 fusion.23
  292.3 4.2 scatter_fusion
  296.5 7.4 gather_fusion
  303.9 1.7 fusion.23
  305.6 4.4 scatter_fusion
  310.0 7.4 gather_fusion
  317.4 1.7 fusion.23
  319.1 4.4 scatter_fusion
  323.5 7.4 gather_fusion
  330.9 1.7 fusion.23
  332.6 4.4 scatter_fusion
  337.0 0.0 reduce-scatter.3.cloned.1.call-update
  337.1 0.0 all-gather.2.cloned.1.call-start
  337.1 55.0 %reduce-scatter.3.cloned.1.call-done = f32[512,512]{1,0:T(8,128)} async-done(((f32[2048,512]{1,0:T(8,128)}), f32[512,512]{1,0:T(8,128)}) %reduce-scatter.3.cloned.1.call-update) | async-done | bytes 1048592 | tf_op jit(solution)/shard_map/reduce_scatter | solution.py:53
  392.1 0.0 copy-done.2
  392.1 0.0 copy-done.4
  392.1 2.8 multiply_convert_fusion.1
  394.9 0.0 all-gather.2.cloned.1.call-update
  394.9 0.0 reduce-scatter.5.cloned.1.call-start
  395.0 30.4 %all-gather.2.cloned.1.call-done = bf16[2048,512]{1,0:T(8,128)(2,1)} async-done(((bf16[512,512]{1,0:T(8,128)(2,1)}), bf16[2048,512]{1,0:T(8,128)(2,1)}) %all-gather.2.cloned.1.call-update) | async-done | bytes 2097168 | tf_op jit(solution)/shard_map/all_gather | solution.py:59
  425.5 7.2 gather_fusion.1
  432.7 0.0 copy-done.1
  432.7 11.5 %convolution_bitcast_fusion = f32[64,128,512]{1,2,0:T(8,128)} fusion(bf16[64,128,512]{2,1,0:T(8,128)(2,1)} %gather_fusion.1, bf16[64,128,128]{2,1,0:T(8,128)(2,1)S(1)} %bitcast.47), kind=kOutput, calls=%fused_computation.17 | convolution fusion | flops 1073741824 | bytes 27262976 | tf_op jit(solution)/shard_map/sji,sjf->sif/dot_general | solution.py:61
  444.2 17.4 %copy.14 = f32[64,128,512]{2,1,0:T(8,128)} copy(f32[64,128,512]{1,2,0:T(8,128)} %convolution_bitcast_fusion) | data formatting | bytes 33554432 | tf_op jit(solution)/shard_map/sji,sjf->sif/dot_general | solution.py:61
  461.6 11.3 %broadcast_in_dim.19 = f32[128,128,512]{2,1,0:T(8,128)} broadcast(f32[]{:T(128)} %constant.5.clone.1), dimensions={} | broadcast | bytes 33554436 | tf_op jit(solution)/shard_map/broadcast_in_dim | solution.py:66
  472.9 36.1 %scatter_fusion.1 = f32[128,128,512]{2,1,0:T(8,128)} fusion(f32[128,128,512]{2,1,0:T(8,128)} %broadcast_in_dim.19, s32[64]{0:T(128)S(1)} %compare_select_fusion.3, f32[64,128,512]{2,1,0:T(8,128)} %copy.14), kind=kCustom, calls=%fused_computation.3 | custom fusion | flops 4194304 | bytes 50331904 | tf_op jit(solution)/shard_map/scatter-add | solution.py:67
  509.0 0.0 reduce-scatter.5.cloned.1.call-update
  509.1 0.0 all-reduce.2.cloned.1.call-start
  509.1 165.5 %reduce-scatter.5.cloned.1.call-done = f32[512,512]{1,0:T(8,128)} async-done(((f32[16384,512]{1,0:T(8,128)}), f32[512,512]{1,0:T(8,128)}) %reduce-scatter.5.cloned.1.call-update) | async-done | bytes 1048592 | tf_op jit(solution)/shard_map/reduce_scatter | solution.py:68
  674.6 2.7 convolution_bitcast_fusion.1
  677.4 0.0 all-reduce.2.cloned.1.call-update
  677.4 0.0 copy-done.3
  677.4 2.5 convolution_convert_fusion
  679.9 147.7 %all-reduce.2.cloned.1.call-done = f32[512,512]{0,1:T(8,128)} async-done(((f32[512,512]{0,1:T(8,128)}), f32[512,512]{0,1:T(8,128)}) %all-reduce.2.cloned.1.call-update) | async-done | bytes 1048592 | tf_op jit(solution)/shard_map/psum | solution.py:81
  827.6 2.5 copy.15
  (23 shorter events, 0.1 us)
Async XLA Ops:
  7.2 1.1 copy-start
  15.7 9.7 %copy-start.5 = (s32[64]{0:T(128)S(1)}, s32[64]{0:T(128)}, u32[]{:S(2)}) copy-start(s32[64]{0:T(128)} %param.14) | copy-start | bytes 772
  15.7 9.8 %copy-start.6 = (s32[64]{0:T(128)S(1)}, s32[64]{0:T(128)}, u32[]{:S(2)}) copy-start(s32[64]{0:T(128)} %param.15) | copy-start | bytes 772
  15.7 211.7 %all-to-all-start = ((bf16[32,512,512]{2,1,0:T(8,128)(2,1)}), bf16[32,512,512]{2,1,0:T(8,128)(2,1)}, u32[]{:S(2)}, u32[]{:S(2)}) async-start(bf16[32,512,512]{2,1,0:T(8,128)(2,1)} %stack.2), calls=%async_computation | async-start | bytes 33554432 | tf_op jit(solution)/shard_map/all_to_all | solution.py:44
  25.3 366.8 %reduce-scatter.3.cloned.1.call-start = ((), (), s32[]{:S(2)}) async-start(), calls=%async_computation.3 | async-start | bytes 5242880 | tf_op jit(solution)/shard_map/reduce_scatter | solution.py:53
  229.8 162.3 %copy-start.2 = (bf16[512,512]{1,0:T(8,128)(2,1)S(1)}, bf16[512,512]{1,0:T(8,128)(2,1)}, u32[]{:S(2)}) copy-start(bf16[512,512]{1,0:T(8,128)(2,1)} %param.17) | copy-start | bytes 1572868
  229.8 162.3 %copy-start.4 = (f32[512]{0:T(512)S(1)}, f32[512]{0:T(512)}, u32[]{:S(2)}) copy-start(f32[512]{0:T(512)} %param.12) | copy-start | bytes 6148
  337.1 88.4 %all-gather.2.cloned.1.call-start = ((), (), s32[]{:S(2)}) async-start(), calls=%async_computation.4 | async-start | bytes 2621440 | tf_op jit(solution)/shard_map/all_gather | solution.py:59
  394.9 279.7 %reduce-scatter.5.cloned.1.call-start = ((), (), s32[]{:S(2)}) async-start(), calls=%async_computation.5 | async-start | bytes 34603008 | tf_op jit(solution)/shard_map/reduce_scatter | solution.py:68
  425.5 7.2 copy-start.1
  509.0 168.3 %copy-start.3 = (bf16[512,512]{1,0:T(8,128)(2,1)S(1)}, bf16[512,512]{1,0:T(8,128)(2,1)}, u32[]{:S(2)}) copy-start(bf16[512,512]{1,0:T(8,128)(2,1)} %param.11) | copy-start | bytes 1572868
  509.1 318.6 %all-reduce.2.cloned.1.call-start = ((), (), s32[]{:S(2)}) async-start(), calls=%async_computation.6 | async-start | bytes 2097152 | tf_op jit(solution)/shard_map/psum | solution.py:81
Sparse Core Ops, SparseCore 0:
  337.2 54.8 reduce-scatter.2
  395.1 30.3 all-gather.1
  509.2 165.3 reduce-scatter.4
  679.8 147.7 all-reduce.1
